TPU v7x, 256 devices: a whole 4x4x8 slice. The times are simulated.
256 devices in a mesh: pool: 4 (over x_hi, core), frame: 16 (over x_lo, z), tensor: 4 (over y).
Axes of the slice: x: 4 (x_hi: 2, x_lo: 2; x = x_hi * 2 + x_lo), y: 4, z: 8, core: 2. Of those that a mesh axis runs over, the one named last changes fastest.
Arguments:
- latents: bfloat16 [32768, 2240], P(('pool', 'frame', 'tensor')), parts along dimension 0, may hold values from -6 to 6
- queries: bfloat16 [32768, 2240], P(('pool', 'frame'), 'tensor'), parts along dimension 0, may hold values from -6 to 6
- keys: bfloat16 [32768, 2240], P(('pool', 'frame'), 'tensor'), parts along dimension 0, may hold values from -6 to 6
- values: bfloat16 [32768, 2240], P(('pool', 'frame'), 'tensor'), parts along dimension 0, may hold values from -6 to 6
- log_decay: float32 [20, 32768], P('tensor', ('pool', 'frame')), parts along dimension 1, may hold values from -0.6 to 0, as said below
- block_ids: int32 [32768], P(('pool', 'frame')), parts along dimension 0, may hold values from 0 to 3, as said below
- t_index: int32 [4], P('pool'), parts along dimension 0, may hold values from 0 to 49
- w_mod: bfloat16 [256, 8960], replicated, may hold values from -0.375 to 0.375
- w_out: bfloat16 [2240, 2240], P('tensor', 'frame'), may hold values from -0.125 to 0.125
- w_up: bfloat16 [2240, 4480], P('frame', 'tensor'), may hold values from -0.125 to 0.125
- w_down: bfloat16 [4480, 2240], P('tensor', 'frame'), may hold values from -0.09375 to 0.09375
Outputs:
- velocity: bfloat16 [32768, 2240], P(('pool', 'frame', 'tensor')), parts along dimension 0
- advanced: bfloat16 [32768, 2240], P(('pool', 'frame', 'tensor')), parts along dimension 0
There are 4 independent parts, one for each index of `pool`. A program takes and returns all parts, laid end to end along the dimension named above; an argument that names none is the same for every part. Nothing has to cross between parts.
Inputs may be any that keep to these rules, and one draw needn't show every extreme that they name: `block_ids`: within each span of 512 tokens the value never falls, starts at 0 and ends at 3. `log_decay`: every entry is negative.
All inputs are finite; a program needn't handle non-finite values.
Results may differ from a plain program's by a relative error of at most 0.0085.
Values may be sent and summed in bfloat16 or wider, within the bound.
No kernel may reach another device: no remote copies, remote signals or barrier semaphores. Data moves between devices by JAX's collectives and lax.ppermute only.
A program may use at most 128 MiB of HBM per device.

v0:
```python
import math
import jax
import jax.numpy as jnp
from jax import lax
from jax.sharding import PartitionSpec as P

STEPS = 50


def shifted(block, axis, distance):
    devices = range(lax.axis_size(axis))
    route = [(i - distance, i) for i in devices if i - distance in devices]
    return lax.ppermute(block, axis, route)


def modulation_of(t_index, w_mod):
    fraction = 1.0 - t_index[0].astype(jnp.float32) / STEPS
    following = fraction - 1.0 / STEPS
    sigma_now = 3.0 * fraction / (1.0 + 2.0 * fraction)
    sigma_next = 3.0 * following / (1.0 + 2.0 * following)
    half_width = w_mod.shape[0] // 2
    frequency = jnp.exp(
        -math.log(10000.0) * jnp.arange(half_width).astype(jnp.float32) / half_width
    )
    angles = 1000.0 * sigma_now * frequency
    embedding = jnp.concatenate([jnp.cos(angles), jnp.sin(angles)])
    time_features = jax.nn.silu(embedding).astype(jnp.bfloat16)
    shifts = jnp.dot(time_features[None, :], w_mod, preferred_element_type=jnp.float32)[0]
    return (shifts, sigma_next - sigma_now)


def own_state(key_heads, value_heads, cumulative):
    block_total = cumulative[:, -1]
    scaled = key_heads.astype(jnp.float32) * jnp.exp(block_total[:, None] - cumulative)[:, :, None]
    state_sum = jnp.einsum(
        "htd,hte->hde", scaled, value_heads.astype(jnp.float32), precision=lax.Precision.HIGHEST
    )
    return (block_total, state_sum)


def mix_block(query_heads, key_heads, value_heads, cumulative, labels, carried_state):
    factor = query_heads.shape[2] ** (-0.5)
    visible = labels[None, :] <= labels[:, None]
    decay = jnp.exp(jnp.minimum(cumulative[:, :, None] - cumulative[:, None, :], 0.0))
    weights = jnp.where(visible[None], decay, 0.0) * factor
    scores = jnp.einsum("hid,hjd->hij", query_heads, key_heads, preferred_element_type=jnp.float32)
    probs = (scores * weights).astype(jnp.bfloat16)
    inner_part = jnp.einsum("hij,hjd->hid", probs, value_heads, preferred_element_type=jnp.float32)
    carried = jnp.einsum(
        "hid,hde->hie",
        query_heads.astype(jnp.float32),
        carried_state,
        precision=lax.Precision.HIGHEST,
    )
    numerator = inner_part + carried * (jnp.exp(cumulative) * factor)[:, :, None]
    normed = numerator * lax.rsqrt(jnp.mean(numerator * numerator, axis=2, keepdims=True) + 1e-06)
    return normed.astype(jnp.bfloat16)


def layer_norm(hidden):
    centered = hidden - jnp.mean(hidden, axis=1, keepdims=True)
    variance = jnp.mean(centered * centered, axis=1, keepdims=True)
    return centered * lax.rsqrt(variance + 1e-06)


def on_device(
    latents, queries, keys, values, log_decay, block_ids, t_index, w_mod, w_out, w_up, w_down
):
    shifts, step_size = modulation_of(t_index, w_mod)
    width = latents.shape[1]
    head_count = log_decay.shape[0]
    token_count = log_decay.shape[1]
    head_size = queries.shape[1] // head_count

    def to_heads(rows_in):
        return rows_in.reshape(token_count, head_count, head_size).transpose(1, 0, 2)

    query_heads = to_heads(queries)
    key_heads = to_heads(keys)
    value_heads = to_heads(values)
    cumulative = jnp.cumsum(log_decay, axis=1)
    block_total, state_sum = own_state(key_heads, value_heads, cumulative)
    keep_factor = jnp.exp(block_total)[:, None, None]

    def relay(turn, incoming):
        return shifted(
            (keep_factor * incoming + state_sum).astype(jnp.bfloat16), "frame", 1
        ).astype(jnp.float32)

    carried_state = lax.fori_loop(0, lax.axis_size("frame") - 1, relay, jnp.zeros_like(state_sum))
    mixed = mix_block(query_heads, key_heads, value_heads, cumulative, block_ids, carried_state)
    mixed_rows = mixed.transpose(1, 0, 2).reshape(token_count, head_count * head_size)
    head_terms = jnp.dot(
        mixed_rows,
        lax.all_gather(w_out, "frame", axis=1, tiled=True),
        preferred_element_type=jnp.float32,
    )
    attention = lax.psum_scatter(
        head_terms.astype(jnp.bfloat16), "tensor", scatter_dimension=0, tiled=True
    ).astype(jnp.float32)
    hidden = latents.astype(jnp.float32) + shifts[3 * width :] * attention
    normed = (layer_norm(hidden) * (1.0 + shifts[width : 2 * width]) + shifts[:width]).astype(
        jnp.bfloat16
    )
    normed_all = lax.all_gather(normed, "tensor", axis=0, tiled=True)
    up_sums = jnp.dot(
        normed_all,
        lax.all_gather(w_up, "frame", axis=0, tiled=True),
        preferred_element_type=jnp.float32,
    )
    units = jax.nn.gelu(up_sums, approximate=True).astype(jnp.bfloat16)
    unit_terms = jnp.dot(
        units,
        lax.all_gather(w_down, "frame", axis=1, tiled=True),
        preferred_element_type=jnp.float32,
    )
    feed = lax.psum_scatter(
        unit_terms.astype(jnp.bfloat16), "tensor", scatter_dimension=0, tiled=True
    ).astype(jnp.float32)
    velocity = (hidden + shifts[2 * width : 3 * width] * feed).astype(jnp.bfloat16)
    advanced = (latents.astype(jnp.float32) + step_size * velocity.astype(jnp.float32)).astype(
        jnp.bfloat16
    )
    return (velocity, advanced)


def solution(mesh):
    return jax.shard_map(
        on_device,
        mesh=mesh,
        in_specs=(
            P(("pool", "frame", "tensor"), None),
            P(("pool", "frame"), "tensor"),
            P(("pool", "frame"), "tensor"),
            P(("pool", "frame"), "tensor"),
            P("tensor", ("pool", "frame")),
            P(("pool", "frame")),
            P("pool"),
            P(),
            P("tensor", "frame"),
            P("frame", "tensor"),
            P("tensor", "frame"),
        ),
        out_specs=(P(("pool", "frame", "tensor"), None), P(("pool", "frame", "tensor"), None)),
        check_vma=False,
    )
```

profile of v0, /device:TPU:1, one launch (start us, length us, event | category | flops | bytes accessed | tf_op | source)
XLA Modules:
  0.0 474.8 jit_solution(17253476656250877932)
XLA Ops:
  11.9 1.9 fusion.25
  13.8 120.2 %while.11 = (s32[]{:T(128)}, f32[5,112,112]{2,1,0:T(8,128)S(1)}, f32[5,1,1]{0,2,1:T(1,128)S(1)}, f32[5,112,112]{2,1,0:T(8,128)S(1)}, s32[]{:T(128)}, /*index=5*/s32[]{:T(128)}) while((s32[]{:T(128)}, f32[5,112,112]{2,1,0:T(8,128)S(1)}, f32[5,1,1]{0,2,1:T(1,128)S(1)}, f32[5,112,112]{2,1,0:T(8,128)S(1)}, s32[]{:T(128)}, ...), condition=%wide.region_3.4_spmd.clone, body=%wide.region_2.3_spmd.clone.sunk | while | flops 313603 | bytes 1505419 | solution.py:90
  13.9 4.4 collective-permute-start
  18.3 2.4 collective-permute-done
  20.9 4.1 collective-permute-start
  25.0 3.9 collective-permute-done
  29.1 5.2 %collective-permute-start = (bf16[5,112,112]{2,1,0:T(8,128)(2,1)S(1)}, bf16[5,112,112]{2,1,0:T(8,128)(2,1)S(1)}, u32[]{:S(2)}, u32[]{:S(2)}) collective-permute-start(bf16[5,112,112]{2,1,0:T(8,128)(2,1)S(1)} %fusion.58), channel_id=1, source_target_pairs={{0,4},{4,8},{8,12},{12,16},{16,20},{20,24},{24,28},{28,32},{32,36}... | collective-permute-start | bytes 376328 | tf_op jit(solution)/shard_map/while/body/eval_jaxpr/ppermute | solution.py:13
  34.2 4.6 collective-permute-done
  39.0 4.1 collective-permute-start
  43.1 4.7 collective-permute-done
  48.0 4.1 collective-permute-start
  52.1 3.6 collective-permute-done
  55.8 4.4 collective-permute-start
  60.2 3.5 collective-permute-done
  63.9 5.8 %collective-permute-start = (bf16[5,112,112]{2,1,0:T(8,128)(2,1)S(1)}, bf16[5,112,112]{2,1,0:T(8,128)(2,1)S(1)}, u32[]{:S(2)}, u32[]{:S(2)}) collective-permute-start(bf16[5,112,112]{2,1,0:T(8,128)(2,1)S(1)} %fusion.58), channel_id=1, source_target_pairs={{0,4},{4,8},{8,12},{12,16},{16,20},{20,24},{24,28},{28,32},{32,36}... | collective-permute-start | bytes 376328 | tf_op jit(solution)/shard_map/while/body/eval_jaxpr/ppermute | solution.py:13
  69.7 3.8 collective-permute-done
  73.6 5.2 %collective-permute-start = (bf16[5,112,112]{2,1,0:T(8,128)(2,1)S(1)}, bf16[5,112,112]{2,1,0:T(8,128)(2,1)S(1)}, u32[]{:S(2)}, u32[]{:S(2)}) collective-permute-start(bf16[5,112,112]{2,1,0:T(8,128)(2,1)S(1)} %fusion.58), channel_id=1, source_target_pairs={{0,4},{4,8},{8,12},{12,16},{16,20},{20,24},{24,28},{28,32},{32,36}... | collective-permute-start | bytes 376328 | tf_op jit(solution)/shard_map/while/body/eval_jaxpr/ppermute | solution.py:13
  78.8 2.3 collective-permute-done
  81.2 5.2 %collective-permute-start = (bf16[5,112,112]{2,1,0:T(8,128)(2,1)S(1)}, bf16[5,112,112]{2,1,0:T(8,128)(2,1)S(1)}, u32[]{:S(2)}, u32[]{:S(2)}) collective-permute-start(bf16[5,112,112]{2,1,0:T(8,128)(2,1)S(1)} %fusion.58), channel_id=1, source_target_pairs={{0,4},{4,8},{8,12},{12,16},{16,20},{20,24},{24,28},{28,32},{32,36}... | collective-permute-start | bytes 376328 | tf_op jit(solution)/shard_map/while/body/eval_jaxpr/ppermute | solution.py:13
  86.4 2.0 collective-permute-done
  88.6 4.4 collective-permute-start
  93.0 2.0 collective-permute-done
  95.2 5.6 %collective-permute-start = (bf16[5,112,112]{2,1,0:T(8,128)(2,1)S(1)}, bf16[5,112,112]{2,1,0:T(8,128)(2,1)S(1)}, u32[]{:S(2)}, u32[]{:S(2)}) collective-permute-start(bf16[5,112,112]{2,1,0:T(8,128)(2,1)S(1)} %fusion.58), channel_id=1, source_target_pairs={{0,4},{4,8},{8,12},{12,16},{16,20},{20,24},{24,28},{28,32},{32,36}... | collective-permute-start | bytes 376328 | tf_op jit(solution)/shard_map/while/body/eval_jaxpr/ppermute | solution.py:13
  100.8 2.0 collective-permute-done
  103.0 5.1 %collective-permute-start = (bf16[5,112,112]{2,1,0:T(8,128)(2,1)S(1)}, bf16[5,112,112]{2,1,0:T(8,128)(2,1)S(1)}, u32[]{:S(2)}, u32[]{:S(2)}) collective-permute-start(bf16[5,112,112]{2,1,0:T(8,128)(2,1)S(1)} %fusion.58), channel_id=1, source_target_pairs={{0,4},{4,8},{8,12},{12,16},{16,20},{20,24},{24,28},{28,32},{32,36}... | collective-permute-start | bytes 376328 | tf_op jit(solution)/shard_map/while/body/eval_jaxpr/ppermute | solution.py:13
  108.1 2.9 collective-permute-done
  111.1 5.6 %collective-permute-start = (bf16[5,112,112]{2,1,0:T(8,128)(2,1)S(1)}, bf16[5,112,112]{2,1,0:T(8,128)(2,1)S(1)}, u32[]{:S(2)}, u32[]{:S(2)}) collective-permute-start(bf16[5,112,112]{2,1,0:T(8,128)(2,1)S(1)} %fusion.58), channel_id=1, source_target_pairs={{0,4},{4,8},{8,12},{12,16},{16,20},{20,24},{24,28},{28,32},{32,36}... | collective-permute-start | bytes 376328 | tf_op jit(solution)/shard_map/while/body/eval_jaxpr/ppermute | solution.py:13
  116.7 3.0 collective-permute-done
  119.9 5.4 %collective-permute-start = (bf16[5,112,112]{2,1,0:T(8,128)(2,1)S(1)}, bf16[5,112,112]{2,1,0:T(8,128)(2,1)S(1)}, u32[]{:S(2)}, u32[]{:S(2)}) collective-permute-start(bf16[5,112,112]{2,1,0:T(8,128)(2,1)S(1)} %fusion.58), channel_id=1, source_target_pairs={{0,4},{4,8},{8,12},{12,16},{16,20},{20,24},{24,28},{28,32},{32,36}... | collective-permute-start | bytes 376328 | tf_op jit(solution)/shard_map/while/body/eval_jaxpr/ppermute | solution.py:13
  125.3 2.0 collective-permute-done
  127.5 4.4 collective-permute-start
  131.9 2.0 collective-permute-done
  134.7 3.9 fusion.17
  139.7 3.2 reshape.183
  142.9 4.4 convolution_convert_fusion.1
  147.3 4.2 copy.26
  153.7 3.0 convolution_reduce_fusion
  156.8 60.6 %reduce-scatter.7.cloned.1.call-done = bf16[128,2240]{1,0:T(8,128)(2,1)} async-done(((bf16[512,2240]{1,0:T(8,128)(2,1)}), bf16[128,2240]{1,0:T(8,128)(2,1)}) %reduce-scatter.7.cloned.1.call-update) | async-done | bytes 573456
  219.6 2.1 add_convert_fusion.1
  222.0 66.8 %all-gather.12.cloned.1.call-done = bf16[16,140,1120]{2,1,0:T(8,128)(2,1)} async-done(((bf16[1,140,1120]{2,1,0:T(8,128)(2,1)}), bf16[16,140,1120]{2,1,0:T(8,128)(2,1)}) %all-gather.12.cloned.1.call-update) | async-done | bytes 5017616 | tf_op jit(solution)/shard_map/all_gather | solution.py:108
  288.7 7.9 %reshape.185 = bf16[2240,1120]{1,0:T(8,128)(2,1)} reshape(bf16[16,140,1120]{2,1,0:T(8,128)(2,1)} %all-gather.12.cloned.1.call-done) | data formatting | bytes 10035200
  296.6 69.5 %all-gather.14.cloned.1.call-done = bf16[16,140,1120]{2,1,0:T(8,128)(2,1)} async-done(((bf16[1,140,1120]{2,1,0:T(8,128)(2,1)}), bf16[16,140,1120]{2,1,0:T(8,128)(2,1)}) %all-gather.14.cloned.1.call-update) | async-done | bytes 5017616 | tf_op jit(solution)/shard_map/all_gather | solution.py:114
  366.1 7.9 %reshape.187 = bf16[2240,1120]{1,0:T(8,128)(2,1)} reshape(bf16[16,140,1120]{2,1,0:T(8,128)(2,1)} %all-gather.14.cloned.1.call-done) | data formatting | bytes 10035200
  374.0 37.2 %all-gather.8.cloned.1.call-done = bf16[512,2240]{0,1:T(8,128)(2,1)} async-done(((bf16[128,2240]{0,1:T(8,128)(2,1)}), bf16[512,2240]{0,1:T(8,128)(2,1)}) %all-gather.8.cloned.1.call-update) | async-done | bytes 2293776 | tf_op jit(solution)/shard_map/all_gather | solution.py:105
  411.1 12.2 %convolution_convert_fusion = bf16[512,2240]{0,1:T(8,128)(2,1)} fusion(bf16[2240,1120]{1,0:T(8,128)(2,1)} %reshape.187, bf16[512,2240]{0,1:T(8,128)(2,1)} %all-gather.8.cloned.1.call-done, bf16[2240,1120]{1,0:T(8,128)(2,1)} %reshape.185), kind=kOutput, calls=%fused_computation.4 | convolution fusion | flops 5144330240 | bytes 14622720 | tf_op jit(solution)/shard_map/dot_general | solution.py:112
  423.3 4.2 copy.28
  427.7 36.8 %reduce-scatter.9.cloned.1.call-done = bf16[128,2240]{1,0:T(8,128)(2,1)} async-done(((bf16[512,2240]{1,0:T(8,128)(2,1)}), bf16[128,2240]{1,0:T(8,128)(2,1)}) %reduce-scatter.9.cloned.1.call-update) | async-done | bytes 573456
  465.8 2.1 fusion.14
  (75 shorter events, 13.6 us)
Async XLA Ops:
  7.2 126.8 %copy-start = (bf16[512,560]{0,1:T(8,128)(2,1)S(1)}, bf16[512,560]{0,1:T(8,128)(2,1)}, u32[]{:S(2)}) copy-start(bf16[512,560]{0,1:T(8,128)(2,1)} %param.14) | copy-start | bytes 1720324
  7.2 132.5 %all-gather.10.cloned.1.call-start = ((), (), s32[]{:S(2)}) async-start(), calls=%async_computation.3 | async-start | bytes 3133440 | tf_op jit(solution)/shard_map/all_gather | solution.py:95
  7.9 209.5 %reduce-scatter.7.cloned.1.call-start = ((), (), s32[]{:S(2)}) async-start(), calls=%async_computation.6 | async-start | bytes 2949120
  13.9 6.8 %collective-permute-start = (bf16[5,112,112]{2,1,0:T(8,128)(2,1)S(1)}, bf16[5,112,112]{2,1,0:T(8,128)(2,1)S(1)}, u32[]{:S(2)}, u32[]{:S(2)}) collective-permute-start(bf16[5,112,112]{2,1,0:T(8,128)(2,1)S(1)} %fusion.58), channel_id=1, source_target_pairs={{0,4},{4,8},{8,12},{12,16},{16,20},{20,24},{24,28},{28,32},{32,36}... | collective-permute-start | bytes 376328 | tf_op jit(solution)/shard_map/while/body/eval_jaxpr/ppermute | solution.py:13
  20.9 8.0 %collective-permute-start = (bf16[5,112,112]{2,1,0:T(8,128)(2,1)S(1)}, bf16[5,112,112]{2,1,0:T(8,128)(2,1)S(1)}, u32[]{:S(2)}, u32[]{:S(2)}) collective-permute-start(bf16[5,112,112]{2,1,0:T(8,128)(2,1)S(1)} %fusion.58), channel_id=1, source_target_pairs={{0,4},{4,8},{8,12},{12,16},{16,20},{20,24},{24,28},{28,32},{32,36}... | collective-permute-start | bytes 376328 | tf_op jit(solution)/shard_map/while/body/eval_jaxpr/ppermute | solution.py:13
  29.1 9.8 %collective-permute-start = (bf16[5,112,112]{2,1,0:T(8,128)(2,1)S(1)}, bf16[5,112,112]{2,1,0:T(8,128)(2,1)S(1)}, u32[]{:S(2)}, u32[]{:S(2)}) collective-permute-start(bf16[5,112,112]{2,1,0:T(8,128)(2,1)S(1)} %fusion.58), channel_id=1, source_target_pairs={{0,4},{4,8},{8,12},{12,16},{16,20},{20,24},{24,28},{28,32},{32,36}... | collective-permute-start | bytes 376328 | tf_op jit(solution)/shard_map/while/body/eval_jaxpr/ppermute | solution.py:13
  39.0 8.9 %collective-permute-start = (bf16[5,112,112]{2,1,0:T(8,128)(2,1)S(1)}, bf16[5,112,112]{2,1,0:T(8,128)(2,1)S(1)}, u32[]{:S(2)}, u32[]{:S(2)}) collective-permute-start(bf16[5,112,112]{2,1,0:T(8,128)(2,1)S(1)} %fusion.58), channel_id=1, source_target_pairs={{0,4},{4,8},{8,12},{12,16},{16,20},{20,24},{24,28},{28,32},{32,36}... | collective-permute-start | bytes 376328 | tf_op jit(solution)/shard_map/while/body/eval_jaxpr/ppermute | solution.py:13
  48.0 7.7 %collective-permute-start = (bf16[5,112,112]{2,1,0:T(8,128)(2,1)S(1)}, bf16[5,112,112]{2,1,0:T(8,128)(2,1)S(1)}, u32[]{:S(2)}, u32[]{:S(2)}) collective-permute-start(bf16[5,112,112]{2,1,0:T(8,128)(2,1)S(1)} %fusion.58), channel_id=1, source_target_pairs={{0,4},{4,8},{8,12},{12,16},{16,20},{20,24},{24,28},{28,32},{32,36}... | collective-permute-start | bytes 376328 | tf_op jit(solution)/shard_map/while/body/eval_jaxpr/ppermute | solution.py:13
  55.8 7.9 %collective-permute-start = (bf16[5,112,112]{2,1,0:T(8,128)(2,1)S(1)}, bf16[5,112,112]{2,1,0:T(8,128)(2,1)S(1)}, u32[]{:S(2)}, u32[]{:S(2)}) collective-permute-start(bf16[5,112,112]{2,1,0:T(8,128)(2,1)S(1)} %fusion.58), channel_id=1, source_target_pairs={{0,4},{4,8},{8,12},{12,16},{16,20},{20,24},{24,28},{28,32},{32,36}... | collective-permute-start | bytes 376328 | tf_op jit(solution)/shard_map/while/body/eval_jaxpr/ppermute | solution.py:13
  63.9 9.6 %collective-permute-start = (bf16[5,112,112]{2,1,0:T(8,128)(2,1)S(1)}, bf16[5,112,112]{2,1,0:T(8,128)(2,1)S(1)}, u32[]{:S(2)}, u32[]{:S(2)}) collective-permute-start(bf16[5,112,112]{2,1,0:T(8,128)(2,1)S(1)} %fusion.58), channel_id=1, source_target_pairs={{0,4},{4,8},{8,12},{12,16},{16,20},{20,24},{24,28},{28,32},{32,36}... | collective-permute-start | bytes 376328 | tf_op jit(solution)/shard_map/while/body/eval_jaxpr/ppermute | solution.py:13
  73.6 7.4 %collective-permute-start = (bf16[5,112,112]{2,1,0:T(8,128)(2,1)S(1)}, bf16[5,112,112]{2,1,0:T(8,128)(2,1)S(1)}, u32[]{:S(2)}, u32[]{:S(2)}) collective-permute-start(bf16[5,112,112]{2,1,0:T(8,128)(2,1)S(1)} %fusion.58), channel_id=1, source_target_pairs={{0,4},{4,8},{8,12},{12,16},{16,20},{20,24},{24,28},{28,32},{32,36}... | collective-permute-start | bytes 376328 | tf_op jit(solution)/shard_map/while/body/eval_jaxpr/ppermute | solution.py:13
  81.2 7.2 %collective-permute-start = (bf16[5,112,112]{2,1,0:T(8,128)(2,1)S(1)}, bf16[5,112,112]{2,1,0:T(8,128)(2,1)S(1)}, u32[]{:S(2)}, u32[]{:S(2)}) collective-permute-start(bf16[5,112,112]{2,1,0:T(8,128)(2,1)S(1)} %fusion.58), channel_id=1, source_target_pairs={{0,4},{4,8},{8,12},{12,16},{16,20},{20,24},{24,28},{28,32},{32,36}... | collective-permute-start | bytes 376328 | tf_op jit(solution)/shard_map/while/body/eval_jaxpr/ppermute | solution.py:13
  88.6 6.4 %collective-permute-start = (bf16[5,112,112]{2,1,0:T(8,128)(2,1)S(1)}, bf16[5,112,112]{2,1,0:T(8,128)(2,1)S(1)}, u32[]{:S(2)}, u32[]{:S(2)}) collective-permute-start(bf16[5,112,112]{2,1,0:T(8,128)(2,1)S(1)} %fusion.58), channel_id=1, source_target_pairs={{0,4},{4,8},{8,12},{12,16},{16,20},{20,24},{24,28},{28,32},{32,36}... | collective-permute-start | bytes 376328 | tf_op jit(solution)/shard_map/while/body/eval_jaxpr/ppermute | solution.py:13
  95.2 7.7 %collective-permute-start = (bf16[5,112,112]{2,1,0:T(8,128)(2,1)S(1)}, bf16[5,112,112]{2,1,0:T(8,128)(2,1)S(1)}, u32[]{:S(2)}, u32[]{:S(2)}) collective-permute-start(bf16[5,112,112]{2,1,0:T(8,128)(2,1)S(1)} %fusion.58), channel_id=1, source_target_pairs={{0,4},{4,8},{8,12},{12,16},{16,20},{20,24},{24,28},{28,32},{32,36}... | collective-permute-start | bytes 376328 | tf_op jit(solution)/shard_map/while/body/eval_jaxpr/ppermute | solution.py:13
  103.0 8.0 %collective-permute-start = (bf16[5,112,112]{2,1,0:T(8,128)(2,1)S(1)}, bf16[5,112,112]{2,1,0:T(8,128)(2,1)S(1)}, u32[]{:S(2)}, u32[]{:S(2)}) collective-permute-start(bf16[5,112,112]{2,1,0:T(8,128)(2,1)S(1)} %fusion.58), channel_id=1, source_target_pairs={{0,4},{4,8},{8,12},{12,16},{16,20},{20,24},{24,28},{28,32},{32,36}... | collective-permute-start | bytes 376328 | tf_op jit(solution)/shard_map/while/body/eval_jaxpr/ppermute | solution.py:13
  111.1 8.7 %collective-permute-start = (bf16[5,112,112]{2,1,0:T(8,128)(2,1)S(1)}, bf16[5,112,112]{2,1,0:T(8,128)(2,1)S(1)}, u32[]{:S(2)}, u32[]{:S(2)}) collective-permute-start(bf16[5,112,112]{2,1,0:T(8,128)(2,1)S(1)} %fusion.58), channel_id=1, source_target_pairs={{0,4},{4,8},{8,12},{12,16},{16,20},{20,24},{24,28},{28,32},{32,36}... | collective-permute-start | bytes 376328 | tf_op jit(solution)/shard_map/while/body/eval_jaxpr/ppermute | solution.py:13
  119.9 7.4 %collective-permute-start = (bf16[5,112,112]{2,1,0:T(8,128)(2,1)S(1)}, bf16[5,112,112]{2,1,0:T(8,128)(2,1)S(1)}, u32[]{:S(2)}, u32[]{:S(2)}) collective-permute-start(bf16[5,112,112]{2,1,0:T(8,128)(2,1)S(1)} %fusion.58), channel_id=1, source_target_pairs={{0,4},{4,8},{8,12},{12,16},{16,20},{20,24},{24,28},{28,32},{32,36}... | collective-permute-start | bytes 376328 | tf_op jit(solution)/shard_map/while/body/eval_jaxpr/ppermute | solution.py:13
  127.5 6.5 %collective-permute-start = (bf16[5,112,112]{2,1,0:T(8,128)(2,1)S(1)}, bf16[5,112,112]{2,1,0:T(8,128)(2,1)S(1)}, u32[]{:S(2)}, u32[]{:S(2)}) collective-permute-start(bf16[5,112,112]{2,1,0:T(8,128)(2,1)S(1)} %fusion.58), channel_id=1, source_target_pairs={{0,4},{4,8},{8,12},{12,16},{16,20},{20,24},{24,28},{28,32},{32,36}... | collective-permute-start | bytes 376328 | tf_op jit(solution)/shard_map/while/body/eval_jaxpr/ppermute | solution.py:13
  151.5 137.2 %all-gather.12.cloned.1.call-start = ((), (), s32[]{:S(2)}) async-start(), calls=%async_computation.4 | async-start | bytes 5640192 | tf_op jit(solution)/shard_map/all_gather | solution.py:108
  152.3 213.8 %all-gather.14.cloned.1.call-start = ((), (), s32[]{:S(2)}) async-start(), calls=%async_computation.5 | async-start | bytes 5640192 | tf_op jit(solution)/shard_map/all_gather | solution.py:114
  152.8 258.3 %all-gather.8.cloned.1.call-start = ((), (), s32[]{:S(2)}) async-start(), calls=%async_computation.2 | async-start | bytes 2867200 | tf_op jit(solution)/shard_map/all_gather | solution.py:105
  156.7 62.1 %copy-start.1 = (bf16[128,2240]{0,1:T(8,128)(2,1)S(1)}, bf16[128,2240]{0,1:T(8,128)(2,1)}, u32[]{:S(2)}) copy-start(bf16[128,2240]{0,1:T(8,128)(2,1)} %param.13) | copy-start | bytes 1720324
  221.7 242.7 %reduce-scatter.9.cloned.1.call-start = ((), (), s32[]{:S(2)}) async-start(), calls=%async_computation.7 | async-start | bytes 2949120
Sparse Core Ops, SparseCore 0:
  9.8 66.7 all-gather.9
  151.6 65.7 reduce-scatter.6
  219.2 69.4 all-gather.11
  290.4 75.6 all-gather.13
  368.3 42.7 all-gather.7
  427.7 36.6 reduce-scatter.8
where the time goes:
time: 476 us; the launch traced here: 475 us
  waiting for transfers between devices  318 us (67%)
  starting transfers between devices  73.3 us (15%)
  local copies, waits for them, and re-layouts  31.4 us (7%)
  matrix products  26.2 us (6%)
  between operations  15 us (3%)
  other arithmetic  10.9 us (2%)
    unnamed x8, waiting for transfers between devices  99.3 us
    ppermute x15, starting transfers between devices, shifted(): return lax.ppermute(block, axis, route)  72.9 us
    all_gather x1, waiting for transfers between devices, on_device(): lax.all_gather(w_down, 'frame', axis=1, tiled=True)  69.5 us
    all_gather x1, waiting for transfers between devices, on_device(): lax.all_gather(w_up, 'frame', axis=0, tiled=True)  66.8 us
    ppermute x15, waiting for transfers between devices, shifted(): return lax.ppermute(block, axis, route)  45 us
    all_gather x1, waiting for transfers between devices, on_device(): normed_all = lax.all_gather(normed, 'tensor', axis=0, tiled=True)  37.2 us
    unnamed x13, local copies, waits for them, and re-layouts  30.3 us
    dot_general x1, matrix products, on_device(): jnp.dot(units, lax.all_gather(w_down, 'frame', axis=1, tiled=True), prefe...  12.2 us
  transfers between devices with their start and end apart: 21, of which 20 were waited for; matrix products, arithmetic and copies ran while one was open for 8% of the time, Pallas kernels for 0%

commit v1 on v0

--- a/solution.py
+++ b/solution.py
@@ -105,7 +105,9 @@
     normed_all = lax.all_gather(normed, "tensor", axis=0, tiled=True)
     up_sums = jnp.dot(
         normed_all,
-        lax.all_gather(w_up, "frame", axis=0, tiled=True),
+        jnp.concatenate(
+            lax.all_to_all(jnp.stack([w_up] * lax.axis_size("frame")), "frame", 0, 0), axis=0
+        ),
         preferred_element_type=jnp.float32,
     )
     units = jax.nn.gelu(up_sums, approximate=True).astype(jnp.bfloat16)

time: 476 us -> 454 us (0.954)
  waiting for transfers between devices: 318 us -> 271 us
  starting transfers between devices: 73.3 us -> 95.3 us
    all_to_all x0 -> x1, waiting for transfers between devices: none -> 81.5 us  [on_device(): lax.all_to_all(jnp.stack([w_up] * lax.axis_size('frame')), 'frame', 0, 0)]
    all_gather x1 -> x0, waiting for transfers between devices: 66.8 us -> none  [on_device(): lax.all_gather(w_up, 'frame', axis=0, tiled=True)]
    all_gather x1, waiting for transfers between devices: 69.5 us -> 38.8 us  [on_device(): lax.all_gather(w_down, 'frame', axis=1, tiled=True)]
    unnamed x8 -> x7, waiting for transfers between devices: 99.3 us -> 74.3 us
    all_to_all x0 -> x1, starting transfers between devices: none -> 22.1 us  [on_device(): lax.all_to_all(jnp.stack([w_up] * lax.axis_size('frame')), 'frame', 0, 0)]
    reshape x1 -> x2, local copies, waits for them, and re-layouts: 0.73 us -> 8.65 us  [the longest x1 7.92 us: on_device(): jnp.concatenate(lax.all_to_all(jnp.stack([w_up] * lax.axis_size('frame'))...]
    unnamed x13 -> x14, local copies, waits for them, and re-layouts: 30.3 us -> 22.6 us
    all_gather x1, waiting for transfers between devices: 37.2 us -> 31.6 us  [on_device(): normed_all = lax.all_gather(normed, 'tensor', axis=0, tiled=True)]
  transfers between devices with their start and end apart: 21 -> 21, of which waited for: 20 -> 20; matrix products, arithmetic and copies ran while one was open for 8% -> 9% of each run, Pallas kernels for 0% -> 0%
where the time goes in v1:
time: 454 us; the launch traced here: 453 us
  waiting for transfers between devices  271 us (60%)
  starting transfers between devices  95.3 us (21%)
  local copies, waits for them, and re-layouts  34.4 us (8%)
  matrix products  26.2 us (6%)
  between operations  14.7 us (3%)
  other arithmetic  10.9 us (2%)
    all_to_all x1, waiting for transfers between devices, on_device(): lax.all_to_all(jnp.stack([w_up] * lax.axis_size('frame')), 'frame', 0, 0)  81.5 us
    unnamed x7, waiting for transfers between devices  74.3 us
    ppermute x15, starting transfers between devices, shifted(): return lax.ppermute(block, axis, route)  72.9 us
    ppermute x15, waiting for transfers between devices, shifted(): return lax.ppermute(block, axis, route)  45 us
    all_gather x1, waiting for transfers between devices, on_device(): lax.all_gather(w_down, 'frame', axis=1, tiled=True)  38.8 us
    all_gather x1, waiting for transfers between devices, on_device(): normed_all = lax.all_gather(normed, 'tensor', axis=0, tiled=True)  31.6 us
    unnamed x14, local copies, waits for them, and re-layouts  22.6 us
    all_to_all x1, starting transfers between devices, on_device(): lax.all_to_all(jnp.stack([w_up] * lax.axis_size('frame')), 'frame', 0, 0)  22.1 us
  transfers between devices with their start and end apart: 21, of which 20 were waited for; matrix products, arithmetic and copies ran while one was open for 9% of the time, Pallas kernels for 0%

profile of v1, /device:TPU:1, one launch (start us, length us, event | category | flops | bytes accessed | tf_op | source)
XLA Modules:
  0.0 453.0 jit_solution(14670788732547613811)
XLA Ops:
  13.8 120.2 %while.11 = (s32[]{:T(128)}, f32[5,112,112]{2,1,0:T(8,128)S(1)}, f32[5,1,1]{0,2,1:T(1,128)S(1)}, f32[5,112,112]{2,1,0:T(8,128)S(1)}, s32[]{:T(128)}, /*index=5*/s32[]{:T(128)}) while((s32[]{:T(128)}, f32[5,112,112]{2,1,0:T(8,128)S(1)}, f32[5,1,1]{0,2,1:T(1,128)S(1)}, f32[5,112,112]{2,1,0:T(8,128)S(1)}, s32[]{:T(128)}, ...), condition=%wide.region_3.4_spmd.clone, body=%wide.region_2.3_spmd.clone.sunk | while | flops 313603 | bytes 1505419 | solution.py:90
  13.9 4.4 collective-permute-start
  18.3 2.4 collective-permute-done
  20.9 4.1 collective-permute-start
  25.0 3.9 collective-permute-done
  29.1 5.2 %collective-permute-start = (bf16[5,112,112]{2,1,0:T(8,128)(2,1)S(1)}, bf16[5,112,112]{2,1,0:T(8,128)(2,1)S(1)}, u32[]{:S(2)}, u32[]{:S(2)}) collective-permute-start(bf16[5,112,112]{2,1,0:T(8,128)(2,1)S(1)} %fusion.58), channel_id=1, source_target_pairs={{0,4},{4,8},{8,12},{12,16},{16,20},{20,24},{24,28},{28,32},{32,36}... | collective-permute-start | bytes 376328 | tf_op jit(solution)/shard_map/while/body/eval_jaxpr/ppermute | solution.py:13
  34.2 4.6 %collective-permute-done = bf16[5,112,112]{2,1,0:T(8,128)(2,1)S(1)} collective-permute-done((bf16[5,112,112]{2,1,0:T(8,128)(2,1)S(1)}, bf16[5,112,112]{2,1,0:T(8,128)(2,1)S(1)}, u32[]{:S(2)}, u32[]{:S(2)}) %collective-permute-start) | collective-permute-done | bytes 125472 | tf_op jit(solution)/shard_map/while/body/eval_jaxpr/ppermute | solution.py:13
  39.0 4.1 collective-permute-start
  43.1 4.7 %collective-permute-done = bf16[5,112,112]{2,1,0:T(8,128)(2,1)S(1)} collective-permute-done((bf16[5,112,112]{2,1,0:T(8,128)(2,1)S(1)}, bf16[5,112,112]{2,1,0:T(8,128)(2,1)S(1)}, u32[]{:S(2)}, u32[]{:S(2)}) %collective-permute-start) | collective-permute-done | bytes 125472 | tf_op jit(solution)/shard_map/while/body/eval_jaxpr/ppermute | solution.py:13
  48.0 4.1 collective-permute-start
  52.1 3.6 collective-permute-done
  55.8 4.4 collective-permute-start
  60.2 3.5 collective-permute-done
  63.9 5.8 %collective-permute-start = (bf16[5,112,112]{2,1,0:T(8,128)(2,1)S(1)}, bf16[5,112,112]{2,1,0:T(8,128)(2,1)S(1)}, u32[]{:S(2)}, u32[]{:S(2)}) collective-permute-start(bf16[5,112,112]{2,1,0:T(8,128)(2,1)S(1)} %fusion.58), channel_id=1, source_target_pairs={{0,4},{4,8},{8,12},{12,16},{16,20},{20,24},{24,28},{28,32},{32,36}... | collective-permute-start | bytes 376328 | tf_op jit(solution)/shard_map/while/body/eval_jaxpr/ppermute | solution.py:13
  69.7 3.8 collective-permute-done
  73.6 5.2 %collective-permute-start = (bf16[5,112,112]{2,1,0:T(8,128)(2,1)S(1)}, bf16[5,112,112]{2,1,0:T(8,128)(2,1)S(1)}, u32[]{:S(2)}, u32[]{:S(2)}) collective-permute-start(bf16[5,112,112]{2,1,0:T(8,128)(2,1)S(1)} %fusion.58), channel_id=1, source_target_pairs={{0,4},{4,8},{8,12},{12,16},{16,20},{20,24},{24,28},{28,32},{32,36}... | collective-permute-start | bytes 376328 | tf_op jit(solution)/shard_map/while/body/eval_jaxpr/ppermute | solution.py:13
  78.8 2.3 collective-permute-done
  81.2 5.2 %collective-permute-start = (bf16[5,112,112]{2,1,0:T(8,128)(2,1)S(1)}, bf16[5,112,112]{2,1,0:T(8,128)(2,1)S(1)}, u32[]{:S(2)}, u32[]{:S(2)}) collective-permute-start(bf16[5,112,112]{2,1,0:T(8,128)(2,1)S(1)} %fusion.58), channel_id=1, source_target_pairs={{0,4},{4,8},{8,12},{12,16},{16,20},{20,24},{24,28},{28,32},{32,36}... | collective-permute-start | bytes 376328 | tf_op jit(solution)/shard_map/while/body/eval_jaxpr/ppermute | solution.py:13
  86.4 2.0 collective-permute-done
  88.6 4.4 collective-permute-start
  93.0 2.0 collective-permute-done
  95.2 5.6 %collective-permute-start = (bf16[5,112,112]{2,1,0:T(8,128)(2,1)S(1)}, bf16[5,112,112]{2,1,0:T(8,128)(2,1)S(1)}, u32[]{:S(2)}, u32[]{:S(2)}) collective-permute-start(bf16[5,112,112]{2,1,0:T(8,128)(2,1)S(1)} %fusion.58), channel_id=1, source_target_pairs={{0,4},{4,8},{8,12},{12,16},{16,20},{20,24},{24,28},{28,32},{32,36}... | collective-permute-start | bytes 376328 | tf_op jit(solution)/shard_map/while/body/eval_jaxpr/ppermute | solution.py:13
  100.8 2.0 collective-permute-done
  103.0 5.1 %collective-permute-start = (bf16[5,112,112]{2,1,0:T(8,128)(2,1)S(1)}, bf16[5,112,112]{2,1,0:T(8,128)(2,1)S(1)}, u32[]{:S(2)}, u32[]{:S(2)}) collective-permute-start(bf16[5,112,112]{2,1,0:T(8,128)(2,1)S(1)} %fusion.58), channel_id=1, source_target_pairs={{0,4},{4,8},{8,12},{12,16},{16,20},{20,24},{24,28},{28,32},{32,36}... | collective-permute-start | bytes 376328 | tf_op jit(solution)/shard_map/while/body/eval_jaxpr/ppermute | solution.py:13
  108.1 2.9 collective-permute-done
  111.1 5.6 %collective-permute-start = (bf16[5,112,112]{2,1,0:T(8,128)(2,1)S(1)}, bf16[5,112,112]{2,1,0:T(8,128)(2,1)S(1)}, u32[]{:S(2)}, u32[]{:S(2)}) collective-permute-start(bf16[5,112,112]{2,1,0:T(8,128)(2,1)S(1)} %fusion.58), channel_id=1, source_target_pairs={{0,4},{4,8},{8,12},{12,16},{16,20},{20,24},{24,28},{28,32},{32,36}... | collective-permute-start | bytes 376328 | tf_op jit(solution)/shard_map/while/body/eval_jaxpr/ppermute | solution.py:13
  116.7 3.0 collective-permute-done
  119.9 5.4 %collective-permute-start = (bf16[5,112,112]{2,1,0:T(8,128)(2,1)S(1)}, bf16[5,112,112]{2,1,0:T(8,128)(2,1)S(1)}, u32[]{:S(2)}, u32[]{:S(2)}) collective-permute-start(bf16[5,112,112]{2,1,0:T(8,128)(2,1)S(1)} %fusion.58), channel_id=1, source_target_pairs={{0,4},{4,8},{8,12},{12,16},{16,20},{20,24},{24,28},{28,32},{32,36}... | collective-permute-start | bytes 376328 | tf_op jit(solution)/shard_map/while/body/eval_jaxpr/ppermute | solution.py:13
  127.5 4.4 collective-permute-start
  131.9 2.0 collective-permute-done
  134.7 3.9 fusion.17
  139.7 3.2 reshape.189
  142.9 4.4 convolution_convert_fusion.1
  147.3 4.3 copy.26
  152.5 2.8 stack.2
  155.3 22.1 %all-to-all-start = ((bf16[16,140,1120]{2,1,0:T(8,128)(2,1)}), bf16[16,140,1120]{2,1,0:T(8,128)(2,1)}, u32[]{:S(2)}, u32[]{:S(2)}) async-start(bf16[16,140,1120]{2,1,0:T(8,128)(2,1)} %stack.2), calls=%async_computation | async-start | bytes 10616832 | tf_op jit(solution)/shard_map/all_to_all | solution.py:109
  178.2 3.0 convolution_reduce_fusion
  181.3 36.1 %reduce-scatter.7.cloned.1.call-done = bf16[128,2240]{1,0:T(8,128)(2,1)} async-done(((bf16[512,2240]{1,0:T(8,128)(2,1)}), bf16[128,2240]{1,0:T(8,128)(2,1)}) %reduce-scatter.7.cloned.1.call-update) | async-done | bytes 573456
  219.6 2.1 add_convert_fusion.1
  222.0 81.5 %all-to-all-done = bf16[16,140,1120]{2,1,0:T(8,128)(2,1)} async-done(((bf16[16,140,1120]{2,1,0:T(8,128)(2,1)}), bf16[16,140,1120]{2,1,0:T(8,128)(2,1)}, u32[]{:S(2)}, u32[]{:S(2)}) %all-to-all-start) | async-done | bytes 5017632 | tf_op jit(solution)/shard_map/all_to_all | solution.py:109
  303.5 7.9 %reshape.178 = bf16[2240,1120]{1,0:T(8,128)(2,1)} reshape(bf16[16,140,1120]{2,1,0:T(8,128)(2,1)} %all-to-all-done) | data formatting | bytes 10035200 | tf_op jit(solution)/shard_map/reshape | solution.py:108
  311.4 38.8 %all-gather.10.cloned.1.call-done = bf16[16,140,1120]{2,1,0:T(8,128)(2,1)} async-done(((bf16[1,140,1120]{2,1,0:T(8,128)(2,1)}), bf16[16,140,1120]{2,1,0:T(8,128)(2,1)}) %all-gather.10.cloned.1.call-update) | async-done | bytes 5017616 | tf_op jit(solution)/shard_map/all_gather | solution.py:116
  350.2 7.9 %reshape.191 = bf16[2240,1120]{1,0:T(8,128)(2,1)} reshape(bf16[16,140,1120]{2,1,0:T(8,128)(2,1)} %all-gather.10.cloned.1.call-done) | data formatting | bytes 10035200
  358.0 31.6 %all-gather.6.cloned.1.call-done = bf16[512,2240]{0,1:T(8,128)(2,1)} async-done(((bf16[128,2240]{0,1:T(8,128)(2,1)}), bf16[512,2240]{0,1:T(8,128)(2,1)}) %all-gather.6.cloned.1.call-update) | async-done | bytes 2293776 | tf_op jit(solution)/shard_map/all_gather | solution.py:105
  389.6 12.2 %convolution_convert_fusion = bf16[512,2240]{0,1:T(8,128)(2,1)} fusion(bf16[2240,1120]{1,0:T(8,128)(2,1)} %reshape.191, bf16[512,2240]{0,1:T(8,128)(2,1)} %all-gather.6.cloned.1.call-done, bf16[2240,1120]{1,0:T(8,128)(2,1)} %reshape.178), kind=kOutput, calls=%fused_computation.4 | convolution fusion | flops 5144330240 | bytes 14622720 | tf_op jit(solution)/shard_map/dot_general | solution.py:114
  401.9 4.2 copy.28
  406.2 36.8 %reduce-scatter.9.cloned.1.call-done = bf16[128,2240]{1,0:T(8,128)(2,1)} async-done(((bf16[512,2240]{1,0:T(8,128)(2,1)}), bf16[128,2240]{1,0:T(8,128)(2,1)}) %reduce-scatter.9.cloned.1.call-update) | async-done | bytes 573456
  444.3 2.1 fusion.14
  (77 shorter events, 17.2 us)
Async XLA Ops:
  7.2 126.8 %copy-start = (bf16[512,560]{0,1:T(8,128)(2,1)S(1)}, bf16[512,560]{0,1:T(8,128)(2,1)}, u32[]{:S(2)}) copy-start(bf16[512,560]{0,1:T(8,128)(2,1)} %param.14) | copy-start | bytes 1720324
  7.2 132.5 %all-gather.8.cloned.1.call-start = ((), (), s32[]{:S(2)}) async-start(), calls=%async_computation.4 | async-start | bytes 3133440 | tf_op jit(solution)/shard_map/all_gather | solution.py:95
  7.9 209.5 %reduce-scatter.7.cloned.1.call-start = ((), (), s32[]{:S(2)}) async-start(), calls=%async_computation.6 | async-start | bytes 2949120
  13.9 6.8 %collective-permute-start = (bf16[5,112,112]{2,1,0:T(8,128)(2,1)S(1)}, bf16[5,112,112]{2,1,0:T(8,128)(2,1)S(1)}, u32[]{:S(2)}, u32[]{:S(2)}) collective-permute-start(bf16[5,112,112]{2,1,0:T(8,128)(2,1)S(1)} %fusion.58), channel_id=1, source_target_pairs={{0,4},{4,8},{8,12},{12,16},{16,20},{20,24},{24,28},{28,32},{32,36}... | collective-permute-start | bytes 376328 | tf_op jit(solution)/shard_map/while/body/eval_jaxpr/ppermute | solution.py:13
  20.9 8.0 %collective-permute-start = (bf16[5,112,112]{2,1,0:T(8,128)(2,1)S(1)}, bf16[5,112,112]{2,1,0:T(8,128)(2,1)S(1)}, u32[]{:S(2)}, u32[]{:S(2)}) collective-permute-start(bf16[5,112,112]{2,1,0:T(8,128)(2,1)S(1)} %fusion.58), channel_id=1, source_target_pairs={{0,4},{4,8},{8,12},{12,16},{16,20},{20,24},{24,28},{28,32},{32,36}... | collective-permute-start | bytes 376328 | tf_op jit(solution)/shard_map/while/body/eval_jaxpr/ppermute | solution.py:13
  29.1 9.8 %collective-permute-start = (bf16[5,112,112]{2,1,0:T(8,128)(2,1)S(1)}, bf16[5,112,112]{2,1,0:T(8,128)(2,1)S(1)}, u32[]{:S(2)}, u32[]{:S(2)}) collective-permute-start(bf16[5,112,112]{2,1,0:T(8,128)(2,1)S(1)} %fusion.58), channel_id=1, source_target_pairs={{0,4},{4,8},{8,12},{12,16},{16,20},{20,24},{24,28},{28,32},{32,36}... | collective-permute-start | bytes 376328 | tf_op jit(solution)/shard_map/while/body/eval_jaxpr/ppermute | solution.py:13
  39.0 8.9 %collective-permute-start = (bf16[5,112,112]{2,1,0:T(8,128)(2,1)S(1)}, bf16[5,112,112]{2,1,0:T(8,128)(2,1)S(1)}, u32[]{:S(2)}, u32[]{:S(2)}) collective-permute-start(bf16[5,112,112]{2,1,0:T(8,128)(2,1)S(1)} %fusion.58), channel_id=1, source_target_pairs={{0,4},{4,8},{8,12},{12,16},{16,20},{20,24},{24,28},{28,32},{32,36}... | collective-permute-start | bytes 376328 | tf_op jit(solution)/shard_map/while/body/eval_jaxpr/ppermute | solution.py:13
  48.0 7.7 %collective-permute-start = (bf16[5,112,112]{2,1,0:T(8,128)(2,1)S(1)}, bf16[5,112,112]{2,1,0:T(8,128)(2,1)S(1)}, u32[]{:S(2)}, u32[]{:S(2)}) collective-permute-start(bf16[5,112,112]{2,1,0:T(8,128)(2,1)S(1)} %fusion.58), channel_id=1, source_target_pairs={{0,4},{4,8},{8,12},{12,16},{16,20},{20,24},{24,28},{28,32},{32,36}... | collective-permute-start | bytes 376328 | tf_op jit(solution)/shard_map/while/body/eval_jaxpr/ppermute | solution.py:13
  55.8 7.9 %collective-permute-start = (bf16[5,112,112]{2,1,0:T(8,128)(2,1)S(1)}, bf16[5,112,112]{2,1,0:T(8,128)(2,1)S(1)}, u32[]{:S(2)}, u32[]{:S(2)}) collective-permute-start(bf16[5,112,112]{2,1,0:T(8,128)(2,1)S(1)} %fusion.58), channel_id=1, source_target_pairs={{0,4},{4,8},{8,12},{12,16},{16,20},{20,24},{24,28},{28,32},{32,36}... | collective-permute-start | bytes 376328 | tf_op jit(solution)/shard_map/while/body/eval_jaxpr/ppermute | solution.py:13
  63.9 9.6 %collective-permute-start = (bf16[5,112,112]{2,1,0:T(8,128)(2,1)S(1)}, bf16[5,112,112]{2,1,0:T(8,128)(2,1)S(1)}, u32[]{:S(2)}, u32[]{:S(2)}) collective-permute-start(bf16[5,112,112]{2,1,0:T(8,128)(2,1)S(1)} %fusion.58), channel_id=1, source_target_pairs={{0,4},{4,8},{8,12},{12,16},{16,20},{20,24},{24,28},{28,32},{32,36}... | collective-permute-start | bytes 376328 | tf_op jit(solution)/shard_map/while/body/eval_jaxpr/ppermute | solution.py:13
  73.6 7.4 %collective-permute-start = (bf16[5,112,112]{2,1,0:T(8,128)(2,1)S(1)}, bf16[5,112,112]{2,1,0:T(8,128)(2,1)S(1)}, u32[]{:S(2)}, u32[]{:S(2)}) collective-permute-start(bf16[5,112,112]{2,1,0:T(8,128)(2,1)S(1)} %fusion.58), channel_id=1, source_target_pairs={{0,4},{4,8},{8,12},{12,16},{16,20},{20,24},{24,28},{28,32},{32,36}... | collective-permute-start | bytes 376328 | tf_op jit(solution)/shard_map/while/body/eval_jaxpr/ppermute | solution.py:13
  81.2 7.2 %collective-permute-start = (bf16[5,112,112]{2,1,0:T(8,128)(2,1)S(1)}, bf16[5,112,112]{2,1,0:T(8,128)(2,1)S(1)}, u32[]{:S(2)}, u32[]{:S(2)}) collective-permute-start(bf16[5,112,112]{2,1,0:T(8,128)(2,1)S(1)} %fusion.58), channel_id=1, source_target_pairs={{0,4},{4,8},{8,12},{12,16},{16,20},{20,24},{24,28},{28,32},{32,36}... | collective-permute-start | bytes 376328 | tf_op jit(solution)/shard_map/while/body/eval_jaxpr/ppermute | solution.py:13
  88.6 6.4 %collective-permute-start = (bf16[5,112,112]{2,1,0:T(8,128)(2,1)S(1)}, bf16[5,112,112]{2,1,0:T(8,128)(2,1)S(1)}, u32[]{:S(2)}, u32[]{:S(2)}) collective-permute-start(bf16[5,112,112]{2,1,0:T(8,128)(2,1)S(1)} %fusion.58), channel_id=1, source_target_pairs={{0,4},{4,8},{8,12},{12,16},{16,20},{20,24},{24,28},{28,32},{32,36}... | collective-permute-start | bytes 376328 | tf_op jit(solution)/shard_map/while/body/eval_jaxpr/ppermute | solution.py:13
  95.2 7.7 %collective-permute-start = (bf16[5,112,112]{2,1,0:T(8,128)(2,1)S(1)}, bf16[5,112,112]{2,1,0:T(8,128)(2,1)S(1)}, u32[]{:S(2)}, u32[]{:S(2)}) collective-permute-start(bf16[5,112,112]{2,1,0:T(8,128)(2,1)S(1)} %fusion.58), channel_id=1, source_target_pairs={{0,4},{4,8},{8,12},{12,16},{16,20},{20,24},{24,28},{28,32},{32,36}... | collective-permute-start | bytes 376328 | tf_op jit(solution)/shard_map/while/body/eval_jaxpr/ppermute | solution.py:13
  103.0 8.0 %collective-permute-start = (bf16[5,112,112]{2,1,0:T(8,128)(2,1)S(1)}, bf16[5,112,112]{2,1,0:T(8,128)(2,1)S(1)}, u32[]{:S(2)}, u32[]{:S(2)}) collective-permute-start(bf16[5,112,112]{2,1,0:T(8,128)(2,1)S(1)} %fusion.58), channel_id=1, source_target_pairs={{0,4},{4,8},{8,12},{12,16},{16,20},{20,24},{24,28},{28,32},{32,36}... | collective-permute-start | bytes 376328 | tf_op jit(solution)/shard_map/while/body/eval_jaxpr/ppermute | solution.py:13
  111.1 8.7 %collective-permute-start = (bf16[5,112,112]{2,1,0:T(8,128)(2,1)S(1)}, bf16[5,112,112]{2,1,0:T(8,128)(2,1)S(1)}, u32[]{:S(2)}, u32[]{:S(2)}) collective-permute-start(bf16[5,112,112]{2,1,0:T(8,128)(2,1)S(1)} %fusion.58), channel_id=1, source_target_pairs={{0,4},{4,8},{8,12},{12,16},{16,20},{20,24},{24,28},{28,32},{32,36}... | collective-permute-start | bytes 376328 | tf_op jit(solution)/shard_map/while/body/eval_jaxpr/ppermute | solution.py:13
  119.9 7.4 %collective-permute-start = (bf16[5,112,112]{2,1,0:T(8,128)(2,1)S(1)}, bf16[5,112,112]{2,1,0:T(8,128)(2,1)S(1)}, u32[]{:S(2)}, u32[]{:S(2)}) collective-permute-start(bf16[5,112,112]{2,1,0:T(8,128)(2,1)S(1)} %fusion.58), channel_id=1, source_target_pairs={{0,4},{4,8},{8,12},{12,16},{16,20},{20,24},{24,28},{28,32},{32,36}... | collective-permute-start | bytes 376328 | tf_op jit(solution)/shard_map/while/body/eval_jaxpr/ppermute | solution.py:13
  127.5 6.5 %collective-permute-start = (bf16[5,112,112]{2,1,0:T(8,128)(2,1)S(1)}, bf16[5,112,112]{2,1,0:T(8,128)(2,1)S(1)}, u32[]{:S(2)}, u32[]{:S(2)}) collective-permute-start(bf16[5,112,112]{2,1,0:T(8,128)(2,1)S(1)} %fusion.58), channel_id=1, source_target_pairs={{0,4},{4,8},{8,12},{12,16},{16,20},{20,24},{24,28},{28,32},{32,36}... | collective-permute-start | bytes 376328 | tf_op jit(solution)/shard_map/while/body/eval_jaxpr/ppermute | solution.py:13
  151.5 1.0 copy-start.2
  151.6 198.6 %all-gather.10.cloned.1.call-start = ((), (), s32[]{:S(2)}) async-start(), calls=%async_computation.5 | async-start | bytes 5640192 | tf_op jit(solution)/shard_map/all_gather | solution.py:116
  155.3 148.2 %all-to-all-start = ((bf16[16,140,1120]{2,1,0:T(8,128)(2,1)}), bf16[16,140,1120]{2,1,0:T(8,128)(2,1)}, u32[]{:S(2)}, u32[]{:S(2)}) async-start(bf16[16,140,1120]{2,1,0:T(8,128)(2,1)} %stack.2), calls=%async_computation | async-start | bytes 10616832 | tf_op jit(solution)/shard_map/all_to_all | solution.py:109
  177.4 212.2 %all-gather.6.cloned.1.call-start = ((), (), s32[]{:S(2)}) async-start(), calls=%async_computation.3 | async-start | bytes 2867200 | tf_op jit(solution)/shard_map/all_gather | solution.py:105
  181.2 37.6 %copy-start.1 = (bf16[128,2240]{0,1:T(8,128)(2,1)S(1)}, bf16[128,2240]{0,1:T(8,128)(2,1)}, u32[]{:S(2)}) copy-start(bf16[128,2240]{0,1:T(8,128)(2,1)} %param.13) | copy-start | bytes 1720324
  221.8 221.2 %reduce-scatter.9.cloned.1.call-start = ((), (), s32[]{:S(2)}) async-start(), calls=%async_computation.7 | async-start | bytes 2949120
Sparse Core Ops, SparseCore 0:
  9.8 66.7 all-gather.7
  151.7 65.7 reduce-scatter.6
  219.2 130.8 all-gather.9
  352.4 37.1 all-gather.5
  406.2 36.6 reduce-scatter.8
